TPU v7x, 256 devices: a whole 4x4x8 slice. The times are simulated.
256 devices in a mesh: fac: 32 (over y, z), scn: 8 (over x, core).
Axes of the slice: x: 4, y: 4, z: 8, core: 2. Of those that a mesh axis runs over, the one named last changes fastest.
Arguments:
- loadings: bfloat16 [196608, 512], P('fac'), may hold values from -0.25 to 0.25
- draws: bfloat16 [512, 6144], P(None, 'scn'), may hold values from -6 to 6
- delta: float32 [196608], P('fac'), may hold values from -0.013671875 to 0.013671875
- gamma: bfloat16 [512, 128, 128], P('fac', 'scn'), may hold values from -0.0014648438 to 0.0014648438
- pair_rows: int32 [512], replicated, may hold values from 0 to 1535, as said below
- pair_cols: int32 [512], replicated, may hold values from 0 to 1535, as said below
- pair_count: int32 [32], replicated, may hold values from 4 to 16, as said below
Outputs:
- pnl: float32 [6144], P('scn')
Inputs may be any that keep to these rules, and one draw needn't show every extreme that they name: Block numbers of the slots; for every owner o, among the 32 entries pair_rows and pair_cols of its slots (live or not), the blocks of each index h of fac (blocks h * 48 to h * 48 + 47) are named at most 2 times, and for every owner some index h is named exactly 2 times. `pair_cols`: see pair_rows; the bound holds with both lists together. An owner's live slots are its first pair_count slots; some owner has all 16 slots live.
All inputs are finite; a program needn't handle non-finite values.
Results may differ from a plain program's by a relative error of at most 0.002.
Values may be sent and summed in bfloat16 or wider, within the bound.
No kernel may reach another device: no remote copies, remote signals or barrier semaphores. Data moves between devices by JAX's collectives and lax.ppermute only.
A program may use at most 128 MiB of HBM per device.

v0:
```python
import jax
import jax.numpy as jnp
from jax import lax
from jax.sharding import PartitionSpec as P


def on_device(loadings, draws, delta, gamma, pair_rows, pair_cols, pair_count):
    owners = lax.axis_size("fac")
    my_index = lax.axis_index("fac")
    capacity = gamma.shape[0]
    block_rows = gamma.shape[2]
    local_blocks = loadings.shape[0] // block_rows
    columns = draws.shape[1]
    per_source = 2 * capacity // owners + 1
    wanted = jnp.stack(
        [pair_rows.reshape(owners, capacity), pair_cols.reshape(owners, capacity)], axis=2
    ).reshape(owners, 2 * capacity)
    source = wanted // local_blocks
    offset = wanted - source * local_blocks
    request_order = jnp.arange(2 * capacity, dtype=jnp.int32)
    same_source = source[:, :, None] == source[:, None, :]
    earlier = request_order[None, :] < request_order[:, None]
    position = jnp.sum((same_source & earlier[None, :, :]).astype(jnp.int32), axis=2)
    slot_index = jnp.arange(per_source, dtype=jnp.int32)
    chosen = (source == my_index)[:, :, None] & (position[:, :, None] == slot_index[None, None, :])
    outgoing = jnp.sum(chosen.astype(jnp.int32) * offset[:, :, None], axis=1).reshape(-1)
    my_source = lax.dynamic_index_in_dim(source, my_index, 0, keepdims=False)
    my_position = lax.dynamic_index_in_dim(position, my_index, 0, keepdims=False)
    arrival = my_source * per_source + my_position
    exposure = jnp.dot(loadings, draws, preferred_element_type=jnp.float32)
    linear = jnp.sum(delta[:, None] * exposure, axis=0)
    shocks = exposure.astype(jnp.bfloat16).reshape(local_blocks, block_rows, columns)
    outbound = shocks[outgoing].reshape(owners, per_source, block_rows, columns)
    inbound = lax.all_to_all(outbound, "fac", split_axis=0, concat_axis=0, tiled=True)
    needed = inbound.reshape(owners * per_source, block_rows, columns)[arrival]
    paired = needed.reshape(capacity, 2, block_rows, columns)
    left_block = paired[:, 0]
    right_block = paired[:, 1]
    my_wanted = lax.dynamic_index_in_dim(wanted, my_index, 0, keepdims=False).reshape(capacity, 2)
    my_count = lax.dynamic_index_in_dim(pair_count, my_index, 0, keepdims=False)
    is_live = (jnp.arange(capacity, dtype=jnp.int32) < my_count).astype(jnp.float32)
    weight = jnp.where(my_wanted[:, 0] == my_wanted[:, 1], 1.0, 2.0).astype(jnp.float32) * is_live
    product = jnp.einsum(
        "cab,cbs->cas",
        lax.all_gather(gamma, "scn", axis=1, tiled=True),
        right_block,
        preferred_element_type=jnp.float32,
    )
    inner = jnp.sum(product * left_block, axis=1)
    quad = jnp.sum(weight[:, None] * inner, axis=0)
    return lax.psum(linear + 0.5 * quad, "fac")


def solution(mesh):
    in_specs = (P("fac", None), P(None, "scn"), P("fac"), P("fac", "scn", None), P(), P(), P())
    out_specs = P("scn")
    return jax.shard_map(
        on_device, mesh=mesh, in_specs=in_specs, out_specs=out_specs, check_vma=False
    )
```

profile of v0, /device:TPU:4, one launch (start us, length us, event | category | flops | bytes accessed | tf_op | source)
XLA Modules:
  0.0 416.4 jit_solution(12494564719701076189)
XLA Ops:
  0.0 0.0 copy-start
  0.0 0.8 stack_reshape.6
  0.8 0.8 stack_reshape.7
  1.6 0.1 copy.24
  1.7 0.1 copy.25
  1.8 0.8 convert_reduce_fusion
  2.6 0.1 select_reduce_fusion
  2.7 0.1 copy.29
  2.8 0.1 reshape.164
  3.0 0.0 copy-done
  3.0 9.3 %fusion.8 = (bf16[6144,768]{1,0:T(8,128)(2,1)}, f32[768]{0:T(1024)S(1)}) fusion(f32[6144]{0:T(1024)} %param.9, bf16[6144,512]{1,0:T(8,128)(2,1)} %param.7, bf16[512,768]{1,0:T(8,128)(2,1)S(1)} %copy-done), kind=kOutput, calls=%fused_computation.36 | convolution fusion | flops 4845992960 | bytes 16542720 | tf_op jit(solution)/shard_map/dot_general | solution.py:30
  12.3 10.7 %gather_fusion = bf16[64,128,768]{2,1,0:T(8,128)(2,1)} fusion(bf16[48,128,768]{2,1,0:T(8,128)(2,1)} %bitcast.32, s32[1024]{0:T(1024)S(1)} %pad_clamp_fusion.1), kind=kCustom, calls=%fused_computation | custom fusion | bytes 25166080 | tf_op jit(solution)/shard_map/gather | solution.py:33
  23.1 11.7 %all-to-all-start = ((bf16[32,2,128,768]{3,2,1,0:T(8,128)(2,1)}), bf16[32,2,128,768]{3,2,1,0:T(8,128)(2,1)}, u32[]{:S(2)}, u32[]{:S(2)}) async-start(bf16[32,2,128,768]{3,2,1,0:T(8,128)(2,1)} %bitcast.31), calls=%async_computation | async-start | bytes 25165824 | tf_op jit(solution)/shard_map/all_to_all | solution.py:34
  34.8 0.2 dynamic-slice_reduce_fusion
  35.0 0.1 reshape.162
  35.0 0.0 copy-done.2
  35.1 0.6 dynamic_slice.14
  35.7 0.8 select_reduce_fusion.1
  36.5 11.9 %all_gather.3 = bf16[16,128,128]{2,1,0:T(8,128)(2,1)S(1)} all-gather(bf16[16,16,128]{2,1,0:T(8,128)(2,1)S(1)} %copy-done.1), channel_id=1, replica_groups=mesh['fac'=32,'scn'=8] {'scn'}, dimensions={1}, use_global_device_ids=true | all-gather | bytes 589824 | tf_op jit(solution)/shard_map/all_gather | solution.py:45
  48.4 267.4 %all-to-all-done = bf16[32,2,128,768]{3,2,1,0:T(8,128)(2,1)} async-done(((bf16[32,2,128,768]{3,2,1,0:T(8,128)(2,1)}), bf16[32,2,128,768]{3,2,1,0:T(8,128)(2,1)}, u32[]{:S(2)}, u32[]{:S(2)}) %all-to-all-start) | async-done | bytes 12582944 | tf_op jit(solution)/shard_map/all_to_all | solution.py:34
  315.8 8.1 %gather_fusion.1 = bf16[32,128,768]{2,1,0:T(8,128)(2,1)} fusion(bf16[64,128,768]{2,1,0:T(8,128)(2,1)} %bitcast.5, s32[1024]{0:T(1024)S(1)} %pad_clamp_fusion), kind=kCustom, calls=%fused_computation.1 | custom fusion | bytes 12583040 | tf_op jit(solution)/shard_map/gather | solution.py:35
  323.9 3.9 fusion
  327.8 0.1 multiply_reduce_fusion.1
  327.9 88.6 %psum.7 = f32[768]{0:T(1024)} all-reduce(f32[768]{0:T(1024)S(1)} %multiply_add_fusion), channel_id=1, replica_groups=mesh['fac'=32,'scn'=8] {'fac'}, use_global_device_ids=true, to_apply=%region_5.6 | all-reduce | flops 768 | bytes 6144 | tf_op jit(solution)/shard_map/psum | solution.py:51
  (12 shorter events, 0.1 us)
Async XLA Ops:
  0.0 3.0 copy-start
  23.1 12.0 %copy-start.2 = (s32[32]{0:T(128)S(1)}, s32[32]{0:T(128)}, u32[]{:S(2)}) copy-start(s32[32]{0:T(128)} %param.13) | copy-start | bytes 388
  23.1 13.4 %copy-start.1 = (bf16[16,16,128]{2,1,0:T(8,128)(2,1)S(1)}, bf16[16,16,128]{2,1,0:T(8,128)(2,1)}, u32[]{:S(2)}) copy-start(bf16[16,16,128]{2,1,0:T(8,128)(2,1)} %param.10) | copy-start | bytes 196612
  23.1 292.7 %all-to-all-start = ((bf16[32,2,128,768]{3,2,1,0:T(8,128)(2,1)}), bf16[32,2,128,768]{3,2,1,0:T(8,128)(2,1)}, u32[]{:S(2)}, u32[]{:S(2)}) async-start(bf16[32,2,128,768]{3,2,1,0:T(8,128)(2,1)} %bitcast.31), calls=%async_computation | async-start | bytes 25165824 | tf_op jit(solution)/shard_map/all_to_all | solution.py:34
where the time goes:
time: 417 us; the launch traced here: 416 us
  waiting for transfers between devices  267 us (64%)
  blocking collectives  100 us (24%)
  local copies, waits for them, and re-layouts  21.7 us (5%)
  matrix products  13.2 us (3%)
  starting transfers between devices  11.7 us (3%)
    all_to_all x1, waiting for transfers between devices, on_device(): lax.all_to_all(outbound, 'fac', split_axis=0, concat_axis=0, tiled=True)  267 us
    psum x1, blocking collectives, on_device(): return lax.psum(linear + 0.5 * quad, 'fac')  88.6 us
    all_gather x1, blocking collectives, on_device(): lax.all_gather(gamma, 'scn', axis=1, tiled=True)  11.9 us
    all_to_all x1, starting transfers between devices, on_device(): lax.all_to_all(outbound, 'fac', split_axis=0, concat_axis=0, tiled=True)  11.7 us
    gather x1, local copies, waits for them, and re-layouts, on_device(): outbound = shocks[outgoing].reshape(owners, per_source, block_rows, columns)  10.7 us
    dot_general x1, matrix products, on_device(): exposure = jnp.dot(loadings, draws, preferred_element_type=jnp.float32)  9.35 us
  transfers between devices with their start and end apart: 1, of which 1 were waited for; matrix products, arithmetic and copies ran while one was open for 0% of the time, Pallas kernels for 0%

commit v1 on v0

--- a/solution.py
+++ b/solution.py
@@ -48,7 +48,7 @@
     )
     inner = jnp.sum(product * left_block, axis=1)
     quad = jnp.sum(weight[:, None] * inner, axis=0)
-    return lax.psum(linear + 0.5 * quad, "fac")
+    return jnp.sum(lax.all_gather(linear + 0.5 * quad, "fac"), axis=0)
 
 
 def solution(mesh):

time: 417 us -> 388 us (0.930)
  blocking collectives: 100 us -> 70.8 us
    psum x1 -> x0, blocking collectives: 88.6 us -> none  [on_device(): return lax.psum(linear + 0.5 * quad, 'fac')]
    all_gather x0 -> x1, blocking collectives: none -> 58.9 us  [on_device(): return jnp.sum(lax.all_gather(linear + 0.5 * quad, 'fac'), axis=0)]
where the time goes in v1:
time: 388 us; the launch traced here: 387 us
  waiting for transfers between devices  267 us (69%)
  blocking collectives  70.8 us (18%)
  local copies, waits for them, and re-layouts  21.7 us (6%)
  matrix products  13.2 us (3%)
  starting transfers between devices  11.7 us (3%)
    all_to_all x1, waiting for transfers between devices, on_device(): lax.all_to_all(outbound, 'fac', split_axis=0, concat_axis=0, tiled=True)  267 us
    all_gather x1, blocking collectives, on_device(): return jnp.sum(lax.all_gather(linear + 0.5 * quad, 'fac'), axis=0)  58.9 us
    all_gather x1, blocking collectives, on_device(): lax.all_gather(gamma, 'scn', axis=1, tiled=True)  11.9 us
    all_to_all x1, starting transfers between devices, on_device(): lax.all_to_all(outbound, 'fac', split_axis=0, concat_axis=0, tiled=True)  11.7 us
    gather x1, local copies, waits for them, and re-layouts, on_device(): outbound = shocks[outgoing].reshape(owners, per_source, block_rows, columns)  10.7 us
    dot_general x1, matrix products, on_device(): exposure = jnp.dot(loadings, draws, preferred_element_type=jnp.float32)  9.35 us
    gather x1, local copies, waits for them, and re-layouts, on_device(): needed = inbound.reshape(owners * per_source, block_rows, columns)[arrival]  8.14 us
  transfers between devices with their start and end apart: 1, of which 1 were waited for; matrix products, arithmetic and copies ran while one was open for 0% of the time, Pallas kernels for 0%

profile of v1, /device:TPU:4, one launch (start us, length us, event | category | flops | bytes accessed | tf_op | source)
XLA Modules:
  0.0 387.5 jit_solution(9488897654049877939)
XLA Ops:
  0.0 0.0 copy-start
  0.0 0.8 stack_reshape.6
  0.8 0.8 stack_reshape.7
  1.6 0.1 copy.32
  1.7 0.1 copy.33
  1.8 0.8 convert_reduce_fusion
  2.6 0.1 select_reduce_fusion
  2.7 0.1 copy.37
  2.8 0.1 reshape.181
  3.0 9.3 %fusion.8 = (bf16[6144,768]{1,0:T(8,128)(2,1)}, f32[768]{0:T(1024)S(1)}) fusion(f32[6144]{0:T(1024)} %param.9, bf16[6144,512]{1,0:T(8,128)(2,1)} %param.7, bf16[512,768]{1,0:T(8,128)(2,1)S(1)} %copy-done), kind=kOutput, calls=%fused_computation.36 | convolution fusion | flops 4845992960 | bytes 16542720 | tf_op jit(solution)/shard_map/dot_general | solution.py:30
  12.3 10.7 %gather_fusion = bf16[64,128,768]{2,1,0:T(8,128)(2,1)} fusion(bf16[48,128,768]{2,1,0:T(8,128)(2,1)} %bitcast.32, s32[1024]{0:T(1024)S(1)} %pad_clamp_fusion.1), kind=kCustom, calls=%fused_computation | custom fusion | bytes 25166080 | tf_op jit(solution)/shard_map/gather | solution.py:33
  23.1 11.7 %all-to-all-start = ((bf16[32,2,128,768]{3,2,1,0:T(8,128)(2,1)}), bf16[32,2,128,768]{3,2,1,0:T(8,128)(2,1)}, u32[]{:S(2)}, u32[]{:S(2)}) async-start(bf16[32,2,128,768]{3,2,1,0:T(8,128)(2,1)} %bitcast.31), calls=%async_computation | async-start | bytes 25165824 | tf_op jit(solution)/shard_map/all_to_all | solution.py:34
  34.8 0.2 dynamic-slice_reduce_fusion
  35.0 0.1 reshape.179
  35.0 0.0 copy-done.2
  35.1 0.6 dynamic_slice.14
  35.7 0.8 select_reduce_fusion.1
  36.5 11.9 %all_gather.7 = bf16[16,128,128]{2,1,0:T(8,128)(2,1)S(1)} all-gather(bf16[16,16,128]{2,1,0:T(8,128)(2,1)S(1)} %copy-done.1), channel_id=1, replica_groups=mesh['fac'=32,'scn'=8] {'scn'}, dimensions={1}, use_global_device_ids=true | all-gather | bytes 589824 | tf_op jit(solution)/shard_map/all_gather | solution.py:45
  48.4 267.4 %all-to-all-done = bf16[32,2,128,768]{3,2,1,0:T(8,128)(2,1)} async-done(((bf16[32,2,128,768]{3,2,1,0:T(8,128)(2,1)}), bf16[32,2,128,768]{3,2,1,0:T(8,128)(2,1)}, u32[]{:S(2)}, u32[]{:S(2)}) %all-to-all-start) | async-done | bytes 12582944 | tf_op jit(solution)/shard_map/all_to_all | solution.py:34
  315.8 8.1 %gather_fusion.1 = bf16[32,128,768]{2,1,0:T(8,128)(2,1)} fusion(bf16[64,128,768]{2,1,0:T(8,128)(2,1)} %bitcast.5, s32[1024]{0:T(1024)S(1)} %pad_clamp_fusion), kind=kCustom, calls=%fused_computation.1 | custom fusion | bytes 12583040 | tf_op jit(solution)/shard_map/gather | solution.py:35
  323.9 3.9 fusion
  327.8 0.1 multiply_reduce_fusion.1
  327.9 58.9 %all-gather.1 = f32[32,1,768]{2,1,0:T(1,128)S(1)} all-gather(f32[1,1,768]{2,1,0:T(1,128)S(1)} %reshape.203), channel_id=2, replica_groups=mesh['fac'=32,'scn'=8] {'fac'}, dimensions={0}, use_global_device_ids=true | all-gather | bytes 101376 | tf_op jit(solution)/shard_map/all_gather | solution.py:51
  386.8 0.7 reduce_sum.59
  (14 shorter events, 0.1 us)
Async XLA Ops:
  0.0 3.0 copy-start
  23.1 12.0 %copy-start.2 = (s32[32]{0:T(128)S(1)}, s32[32]{0:T(128)}, u32[]{:S(2)}) copy-start(s32[32]{0:T(128)} %param.13) | copy-start | bytes 388
  23.1 13.4 %copy-start.1 = (bf16[16,16,128]{2,1,0:T(8,128)(2,1)S(1)}, bf16[16,16,128]{2,1,0:T(8,128)(2,1)}, u32[]{:S(2)}) copy-start(bf16[16,16,128]{2,1,0:T(8,128)(2,1)} %param.10) | copy-start | bytes 196612
  23.1 292.7 %all-to-all-start = ((bf16[32,2,128,768]{3,2,1,0:T(8,128)(2,1)}), bf16[32,2,128,768]{3,2,1,0:T(8,128)(2,1)}, u32[]{:S(2)}, u32[]{:S(2)}) async-start(bf16[32,2,128,768]{3,2,1,0:T(8,128)(2,1)} %bitcast.31), calls=%async_computation | async-start | bytes 25165824 | tf_op jit(solution)/shard_map/all_to_all | solution.py:34
